TPU v7x, 32 devices: a whole 2x2x4 slice. The times are simulated.
32 devices in a mesh: row: 4 (over y, x), col: 8 (over z, core).
Axes of the slice: x: 2, y: 2, z: 4, core: 2. Of those that a mesh axis runs over, the one named last changes fastest.
Arguments:
- hist_corr: float32 [16384, 16384], P('row', 'col'), may hold values from -1 to 1
- hist_resp: float32 [16384, 16384], P('row', 'col'), may hold values from -1 to 1, as said below
- row_corr: float32 [128, 16384], P(None, 'col'), may hold values from -1 to 1
- row_resp: float32 [128, 16384], P(None, 'col'), may hold values from -1 to 1
Outputs:
- final_corr: float32 [128, 16384], P(None, 'col')
- final_resp: float32 [128, 16384], P(None, 'col')
Inputs may be any that keep to these rules, and one draw needn't show every extreme that they name: hist_resp[s, u] is 0 where u > s and 1 where u == s.
All inputs are finite; a program needn't handle non-finite values.
Results may differ from a plain program's by a relative error of at most 0.00015.
Values sent between devices are 32-bit elements; how exact they have to be, the bound alone decides.
A program may use at most 128 MiB of HBM per device.

v0:
```python
import math
import jax
import jax.numpy as jnp
from jax import lax
from jax.sharding import PartitionSpec as P

HIST = 16384
BLOCKS = 4
step_size = 0.2
heat_reservoir_warmth = 0.6


def turn_rows(values):
    row_count = lax.axis_size("row")
    col_count = lax.axis_size("col")
    my_row = lax.axis_index("row")
    piece_span = values.shape[1] // row_count
    piece = lax.dynamic_slice_in_dim(values, my_row * piece_span, piece_span, 1)
    spread = jnp.broadcast_to(piece[None, None], (col_count, 1) + piece.shape)
    moved = lax.all_to_all(
        lax.all_to_all(spread, "col", split_axis=0, concat_axis=1, tiled=True),
        "row",
        split_axis=1,
        concat_axis=0,
        tiled=True,
    )
    return jnp.transpose(moved, (2, 1, 0, 3)).reshape(piece.shape[0], -1)


def turn_cols(values):
    row_count = lax.axis_size("row")
    col_count = lax.axis_size("col")
    my_col = lax.axis_index("col")
    factor = col_count // row_count
    block_span = values.shape[1] // factor
    piece_span = block_span // col_count
    blocks = values.reshape(values.shape[0], factor, block_span)
    piece = lax.dynamic_slice_in_dim(blocks, my_col * piece_span, piece_span, 2)
    ordered = jnp.transpose(piece, (1, 0, 2))
    spread = jnp.broadcast_to(ordered[None], (row_count,) + ordered.shape)
    moved = lax.all_to_all(
        lax.all_to_all(spread, "row", split_axis=0, concat_axis=1, tiled=True),
        "col",
        split_axis=1,
        concat_axis=0,
        tiled=True,
    )
    return jnp.transpose(moved[:, 0], (1, 0, 2)).reshape(values.shape[0], -1)


def energy_layout(values):
    return turn_rows(values)


def cross_layout(values):
    return turn_cols(values)


def advance(
    autocovariance_curve,
    perturbation_reaction,
    memory_corr,
    memory_resp,
    cross_term,
    norm_enforcing_scalar,
    integration_coefficient,
):
    next_corr = autocovariance_curve + step_size * (
        integration_coefficient * (memory_corr + cross_term)
        - norm_enforcing_scalar * autocovariance_curve
    )
    next_resp = perturbation_reaction + step_size * (
        integration_coefficient * memory_resp - norm_enforcing_scalar * perturbation_reaction
    )
    return (next_corr, next_resp)


def body(hist_corr, hist_resp, row_corr, row_resp):
    highest = lax.Precision.HIGHEST
    integration_coefficient = 1.0 / math.sqrt(HIST)
    autocovariance_curve = row_corr
    perturbation_reaction = row_resp
    for block_index in range(BLOCKS):
        history_integrand = 3.0 * autocovariance_curve * perturbation_reaction
        slope_contribution = 1.5 * autocovariance_curve * autocovariance_curve
        multiplier_terms = jnp.sum(
            history_integrand * autocovariance_curve + slope_contribution * perturbation_reaction,
            axis=1,
        )
        part_cross = lax.dot_general(
            slope_contribution,
            hist_resp,
            (((1,), (1,)), ((), ())),
            precision=highest,
            preferred_element_type=jnp.float32,
        )
        enforcing_scalar_sum = lax.psum(multiplier_terms, "col")
        energy_rows = energy_layout(history_integrand)
        cross_total = lax.psum(part_cross, "col")
        cross_term = cross_layout(cross_total)
        norm_enforcing_scalar = (
            heat_reservoir_warmth + integration_coefficient * enforcing_scalar_sum[:, None]
        )
        part_corr = jnp.dot(
            energy_rows, hist_corr, precision=highest, preferred_element_type=jnp.float32
        )
        part_resp = jnp.dot(
            energy_rows, hist_resp, precision=highest, preferred_element_type=jnp.float32
        )
        memory_corr, memory_resp = lax.psum((part_corr, part_resp), "row")
        autocovariance_curve, perturbation_reaction = advance(
            autocovariance_curve,
            perturbation_reaction,
            memory_corr,
            memory_resp,
            cross_term,
            norm_enforcing_scalar,
            integration_coefficient,
        )
    return (autocovariance_curve, perturbation_reaction)


def solution(mesh):
    in_specs = (P("row", "col"), P("row", "col"), P(None, "col"), P(None, "col"))
    out_specs = (P(None, "col"), P(None, "col"))
    return jax.shard_map(body, mesh=mesh, in_specs=in_specs, out_specs=out_specs, check_vma=False)
```

profile of v0, /device:TPU:0, one launch (start us, length us, event | category | flops | bytes accessed | tf_op | source)
XLA Modules:
  0.0 1180.2 jit_solution(5139241333706496647)
XLA Ops:
  10.2 55.3 %all_to_all.180 = f32[8,1,128,512]{3,2,1,0:T(8,128)} all-to-all(f32[8,1,128,512]{3,2,1,0:T(8,128)S(1)} %broadcast_in_dim.16), channel_id=1, replica_groups=mesh['row'=4,'col'=8] {'col'}, dimensions={0} | all-to-all | bytes 4194304 | tf_op jit(solution)/shard_map/all_to_all | solution.py:21
  65.5 4.6 all-to-all-start.1
  70.1 37.2 %fusion = f32[128,4096]{1,0:T(8,128)S(1)} fusion(f32[4096,2048]{1,0:T(8,128)} %param.5, f32[128,2048]{1,0:T(8,128)S(1)} %copy-done.4), kind=kOutput, calls=%fused_computation.20 | convolution fusion | flops 12885426176 | bytes 36700160 | tf_op jit(solution)/shard_map/dot_general | solution.py:90
  110.3 64.6 %all-reduce.13.cloned.1.call-done = f32[128,2,2048]{2,1,0:T(2,128)} async-done(((f32[128,2,2048]{2,1,0:T(2,128)}), f32[128,2,2048]{2,1,0:T(2,128)}) %all-reduce.13.cloned.1.call-update) | async-done | bytes 2097168 | tf_op jit(solution)/shard_map/psum | solution.py:99
  183.6 22.4 %fusion.13 = f32[128,2048]{1,0:T(8,128)} fusion(f32[128,4096]{0,1:T(8,128)S(1)} %bitcast.88, f32[4096,2048]{1,0:T(8,128)} %param.5), kind=kOutput, calls=%fused_computation.45 | convolution fusion | flops 12884901888 | bytes 36700160 | tf_op jit(solution)/shard_map/dot_general | solution.py:107
  206.0 22.4 %fusion.12 = f32[128,2048]{1,0:T(8,128)} fusion(f32[128,4096]{0,1:T(8,128)S(1)} %bitcast.89, f32[4096,2048]{1,0:T(8,128)} %param.4), kind=kOutput, calls=%fused_computation.44 | convolution fusion | flops 12884901888 | bytes 36700160 | tf_op jit(solution)/shard_map/dot_general | solution.py:104
  234.3 29.3 %psum.114 = f32[128]{0:T(128)S(1)} all-reduce(f32[128]{0:T(128)S(1)} %get-tuple-element.20), channel_id=1, replica_groups=mesh['row'=4,'col'=8] {'col'}, use_global_device_ids=true, to_apply=%region_3.0 | all-reduce | flops 128 | bytes 1024 | tf_op jit(solution)/shard_map/psum | solution.py:97
  264.8 33.0 %all-reduce.27.cloned.1.call-done = (f32[128,2048]{1,0:T(8,128)}, f32[128,2048]{1,0:T(8,128)}) async-done(((f32[128,2048]{1,0:T(8,128)}, f32[128,2048]{1,0:T(8,128)}), (f32[128,2048]{1,0:T(8,128)}, f32[128,2048]{1,0:T(8,128)})) %all-reduce.27.cloned.1.call-update) | async-done | bytes 2097168 | tf_op jit(solution)/shard_map/psum | solution.py:110
  301.2 53.5 %all_to_all.181 = f32[8,1,128,512]{3,2,1,0:T(8,128)} all-to-all(f32[8,1,128,512]{3,2,1,0:T(8,128)S(1)} %broadcast_in_dim.18), channel_id=1, replica_groups=mesh['row'=4,'col'=8] {'col'}, dimensions={0} | all-to-all | bytes 4194304 | tf_op jit(solution)/shard_map/all_to_all | solution.py:21
  354.8 4.5 all-to-all-start.5
  359.5 39.0 %fusion.1 = f32[128,4096]{1,0:T(8,128)} fusion(f32[4096,2048]{1,0:T(8,128)} %param.5, f32[128,2048]{1,0:T(8,128)S(1)} %get-tuple-element.18), kind=kOutput, calls=%fused_computation.21 | convolution fusion | flops 12885426176 | bytes 36700160 | tf_op jit(solution)/shard_map/dot_general | solution.py:90
  402.5 64.6 %all-reduce.15.cloned.1.call-done = f32[128,2,2048]{2,1,0:T(2,128)} async-done(((f32[128,2,2048]{2,1,0:T(2,128)}), f32[128,2,2048]{2,1,0:T(2,128)}) %all-reduce.15.cloned.1.call-update) | async-done | bytes 2097168 | tf_op jit(solution)/shard_map/psum | solution.py:99
  476.0 22.4 %fusion.15 = f32[128,2048]{1,0:T(8,128)} fusion(f32[128,4096]{0,1:T(8,128)S(1)} %bitcast.90, f32[4096,2048]{1,0:T(8,128)} %param.5), kind=kOutput, calls=%fused_computation.47 | convolution fusion | flops 12884901888 | bytes 36700160 | tf_op jit(solution)/shard_map/dot_general | solution.py:107
  498.4 22.4 %fusion.14 = f32[128,2048]{1,0:T(8,128)} fusion(f32[128,4096]{0,1:T(8,128)S(1)} %bitcast.91, f32[4096,2048]{1,0:T(8,128)} %param.4), kind=kOutput, calls=%fused_computation.46 | convolution fusion | flops 12884901888 | bytes 36700160 | tf_op jit(solution)/shard_map/dot_general | solution.py:104
  526.9 29.3 %psum.118 = f32[128]{0:T(128)S(1)} all-reduce(f32[128]{0:T(128)S(1)} %get-tuple-element.16), channel_id=1, replica_groups=mesh['row'=4,'col'=8] {'col'}, use_global_device_ids=true, to_apply=%region_8.0 | all-reduce | flops 128 | bytes 1024 | tf_op jit(solution)/shard_map/psum | solution.py:97
  557.3 32.9 %all-reduce.25.cloned.1.call-done = (f32[128,2048]{1,0:T(8,128)}, f32[128,2048]{1,0:T(8,128)}) async-done(((f32[128,2048]{1,0:T(8,128)}, f32[128,2048]{1,0:T(8,128)}), (f32[128,2048]{1,0:T(8,128)}, f32[128,2048]{1,0:T(8,128)})) %all-reduce.25.cloned.1.call-update) | async-done | bytes 2097168 | tf_op jit(solution)/shard_map/psum | solution.py:110
  593.9 53.5 %all_to_all.182 = f32[8,1,128,512]{3,2,1,0:T(8,128)} all-to-all(f32[8,1,128,512]{3,2,1,0:T(8,128)S(1)} %broadcast_in_dim.20), channel_id=1, replica_groups=mesh['row'=4,'col'=8] {'col'}, dimensions={0} | all-to-all | bytes 4194304 | tf_op jit(solution)/shard_map/all_to_all | solution.py:21
  647.4 4.5 all-to-all-start.9
  652.1 37.2 %fusion.2 = f32[128,4096]{1,0:T(8,128)S(1)} fusion(f32[4096,2048]{1,0:T(8,128)} %param.5, f32[128,2048]{1,0:T(8,128)S(1)} %get-tuple-element.15), kind=kOutput, calls=%fused_computation.22 | convolution fusion | flops 12885426176 | bytes 36700160 | tf_op jit(solution)/shard_map/dot_general | solution.py:90
  692.2 64.6 %all-reduce.17.cloned.1.call-done = f32[128,2,2048]{2,1,0:T(2,128)} async-done(((f32[128,2,2048]{2,1,0:T(2,128)}), f32[128,2,2048]{2,1,0:T(2,128)}) %all-reduce.17.cloned.1.call-update) | async-done | bytes 2097168 | tf_op jit(solution)/shard_map/psum | solution.py:99
  765.5 22.4 %fusion.17 = f32[128,2048]{1,0:T(8,128)} fusion(f32[128,4096]{0,1:T(8,128)S(1)} %bitcast.92, f32[4096,2048]{1,0:T(8,128)} %param.5), kind=kOutput, calls=%fused_computation.49 | convolution fusion | flops 12884901888 | bytes 36700160 | tf_op jit(solution)/shard_map/dot_general | solution.py:107
  788.0 22.4 %fusion.16 = f32[128,2048]{1,0:T(8,128)} fusion(f32[128,4096]{0,1:T(8,128)S(1)} %bitcast.93, f32[4096,2048]{1,0:T(8,128)} %param.4), kind=kOutput, calls=%fused_computation.48 | convolution fusion | flops 12884901888 | bytes 36700160 | tf_op jit(solution)/shard_map/dot_general | solution.py:104
  816.4 29.3 %psum.122 = f32[128]{0:T(128)S(1)} all-reduce(f32[128]{0:T(128)S(1)} %get-tuple-element.13), channel_id=1, replica_groups=mesh['row'=4,'col'=8] {'col'}, use_global_device_ids=true, to_apply=%region_13.0 | all-reduce | flops 128 | bytes 1024 | tf_op jit(solution)/shard_map/psum | solution.py:97
  846.9 32.9 %all-reduce.23.cloned.1.call-done = (f32[128,2048]{1,0:T(8,128)}, f32[128,2048]{1,0:T(8,128)}) async-done(((f32[128,2048]{1,0:T(8,128)}, f32[128,2048]{1,0:T(8,128)}), (f32[128,2048]{1,0:T(8,128)}, f32[128,2048]{1,0:T(8,128)})) %all-reduce.23.cloned.1.call-update) | async-done | bytes 2097168 | tf_op jit(solution)/shard_map/psum | solution.py:110
  883.4 53.5 %all_to_all.183 = f32[8,1,128,512]{3,2,1,0:T(8,128)} all-to-all(f32[8,1,128,512]{3,2,1,0:T(8,128)S(1)} %broadcast_in_dim.22), channel_id=1, replica_groups=mesh['row'=4,'col'=8] {'col'}, dimensions={0} | all-to-all | bytes 4194304 | tf_op jit(solution)/shard_map/all_to_all | solution.py:21
  936.9 4.5 all-to-all-start.13
  941.9 37.3 %fusion.3 = f32[128,4096]{1,0:T(8,128)S(1)} fusion(f32[4096,2048]{1,0:T(8,128)} %param.5, f32[128,2048]{1,0:T(8,128)S(1)} %get-tuple-element.12), kind=kOutput, calls=%fused_computation.23 | convolution fusion | flops 12885426176 | bytes 36700160 | tf_op jit(solution)/shard_map/dot_general | solution.py:90
  982.0 64.6 %all-reduce.19.cloned.1.call-done = f32[128,2,2048]{2,1,0:T(2,128)} async-done(((f32[128,2,2048]{2,1,0:T(2,128)}), f32[128,2,2048]{2,1,0:T(2,128)}) %all-reduce.19.cloned.1.call-update) | async-done | bytes 2097168 | tf_op jit(solution)/shard_map/psum | solution.py:99
  1054.6 22.4 %fusion.19 = f32[128,2048]{1,0:T(8,128)} fusion(f32[128,4096]{0,1:T(8,128)S(1)} %bitcast.94, f32[4096,2048]{1,0:T(8,128)} %param.5), kind=kOutput, calls=%fused_computation.51 | convolution fusion | flops 12884901888 | bytes 36700160 | tf_op jit(solution)/shard_map/dot_general | solution.py:107
  1077.0 22.4 %fusion.18 = f32[128,2048]{1,0:T(8,128)} fusion(f32[128,4096]{0,1:T(8,128)S(1)} %bitcast.95, f32[4096,2048]{1,0:T(8,128)} %param.4), kind=kOutput, calls=%fused_computation.50 | convolution fusion | flops 12884901888 | bytes 36700160 | tf_op jit(solution)/shard_map/dot_general | solution.py:104
  1104.3 29.3 %psum.126 = f32[128]{0:T(128)S(1)} all-reduce(f32[128]{0:T(128)S(1)} %get-tuple-element.10), channel_id=1, replica_groups=mesh['row'=4,'col'=8] {'col'}, use_global_device_ids=true, to_apply=%region_18.0 | all-reduce | flops 128 | bytes 1024 | tf_op jit(solution)/shard_map/psum | solution.py:97
  1134.7 34.2 %all-reduce.21.cloned.1.call-done = (f32[128,2048]{1,0:T(8,128)}, f32[128,2048]{1,0:T(8,128)}) async-done(((f32[128,2048]{1,0:T(8,128)}, f32[128,2048]{1,0:T(8,128)}), (f32[128,2048]{1,0:T(8,128)}, f32[128,2048]{1,0:T(8,128)})) %all-reduce.21.cloned.1.call-update) | async-done | bytes 2097168 | tf_op jit(solution)/shard_map/psum | solution.py:110
  (98 shorter events, 91.2 us)
Async XLA Ops:
  65.5 4.7 copy-start.4
  65.5 110.4 %all-to-all-start.1 = ((f32[1,8,128,512]{3,2,0,1:T(8,128)}), f32[1,8,128,512]{3,2,0,1:T(8,128)}, u32[]{:S(2)}, u32[]{:S(2)}) async-start(f32[1,8,128,512]{3,2,0,1:T(8,128)} %bitcast.1), calls=%async_computation.1 | async-start | bytes 4194304 | tf_op jit(solution)/shard_map/all_to_all | solution.py:20
  70.1 104.8 %all-reduce.13.cloned.1.call-start = ((), (), s32[]{:S(2)}) async-start(), calls=%async_computation.16 | async-start | bytes 4194304 | tf_op jit(solution)/shard_map/psum | solution.py:99
  177.2 51.3 %all-to-all-start.2 = ((f32[4,2,128,256]{3,1,2,0:T(2,128)}), f32[4,2,128,256]{3,1,2,0:T(2,128)}, u32[]{:S(2)}, u32[]{:S(2)}) async-start(f32[4,2,128,256]{3,1,2,0:T(2,128)} %broadcast_in_dim.17), calls=%async_computation.2 | async-start | bytes 2097152 | tf_op jit(solution)/shard_map/all_to_all | solution.py:42
  181.4 116.4 %all-reduce.27.cloned.1.call-start = ((), (), s32[]{:S(2)}) async-start(), calls=%async_computation.23 | async-start | bytes 4194304 | tf_op jit(solution)/shard_map/psum | solution.py:110
  230.8 32.9 %all-to-all-start.3 = ((f32[1,8,128,256]{3,2,0,1:T(8,128)}), f32[1,8,128,256]{3,2,0,1:T(8,128)S(1)}, u32[]{:S(2)}, u32[]{:S(2)}) async-start(f32[1,8,128,256]{3,2,0,1:T(8,128)} %bitcast.7), calls=%async_computation.3 | async-start | bytes 2097152 | tf_op jit(solution)/shard_map/all_to_all | solution.py:41
  300.8 58.7 %copy-start = (f32[128,2048]{1,0:T(8,128)}, f32[128,2048]{1,0:T(8,128)S(1)}, u32[]{:S(2)}) copy-start(f32[128,2048]{1,0:T(8,128)S(1)} %get-tuple-element.18) | copy-start | bytes 3145732
  354.8 113.3 %all-to-all-start.5 = ((f32[1,8,128,512]{3,2,0,1:T(8,128)}), f32[1,8,128,512]{3,2,0,1:T(8,128)}, u32[]{:S(2)}, u32[]{:S(2)}) async-start(f32[1,8,128,512]{3,2,0,1:T(8,128)} %bitcast.96), calls=%async_computation.5 | async-start | bytes 4194304 | tf_op jit(solution)/shard_map/all_to_all | solution.py:20
  359.2 107.9 %all-reduce.15.cloned.1.call-start = ((), (), s32[]{:S(2)}) async-start(), calls=%async_computation.17 | async-start | bytes 4194304 | tf_op jit(solution)/shard_map/psum | solution.py:99
  469.3 51.5 %all-to-all-start.6 = ((f32[4,2,128,256]{3,1,2,0:T(2,128)}), f32[4,2,128,256]{3,1,2,0:T(2,128)}, u32[]{:S(2)}, u32[]{:S(2)}) async-start(f32[4,2,128,256]{3,1,2,0:T(2,128)} %broadcast_in_dim.19), calls=%async_computation.6 | async-start | bytes 2097152 | tf_op jit(solution)/shard_map/all_to_all | solution.py:42
  473.6 116.6 %all-reduce.25.cloned.1.call-start = ((), (), s32[]{:S(2)}) async-start(), calls=%async_computation.22 | async-start | bytes 4194304 | tf_op jit(solution)/shard_map/psum | solution.py:110
  523.2 67.0 %copy-start.1 = (f32[128,2048]{1,0:T(8,128)S(1)}, f32[128,2048]{1,0:T(8,128)}, u32[]{:S(2)}) copy-start(f32[128,2048]{1,0:T(8,128)} %copy-done) | copy-start | bytes 3145732
  523.2 33.0 %all-to-all-start.7 = ((f32[1,8,128,256]{3,2,0,1:T(8,128)}), f32[1,8,128,256]{3,2,0,1:T(8,128)S(1)}, u32[]{:S(2)}, u32[]{:S(2)}) async-start(f32[1,8,128,256]{3,2,0,1:T(8,128)} %bitcast.101), calls=%async_computation.7 | async-start | bytes 2097152 | tf_op jit(solution)/shard_map/all_to_all | solution.py:41
  592.9 1.0 copy-start.5
  647.4 110.4 %all-to-all-start.9 = ((f32[1,8,128,512]{3,2,0,1:T(8,128)}), f32[1,8,128,512]{3,2,0,1:T(8,128)}, u32[]{:S(2)}, u32[]{:S(2)}) async-start(f32[1,8,128,512]{3,2,0,1:T(8,128)} %bitcast.21), calls=%async_computation.9 | async-start | bytes 4194304 | tf_op jit(solution)/shard_map/all_to_all | solution.py:20
  651.8 105.0 %all-reduce.17.cloned.1.call-start = ((), (), s32[]{:S(2)}) async-start(), calls=%async_computation.18 | async-start | bytes 4194304 | tf_op jit(solution)/shard_map/psum | solution.py:99
  759.1 51.3 %all-to-all-start.10 = ((f32[4,2,128,256]{3,1,2,0:T(2,128)}), f32[4,2,128,256]{3,1,2,0:T(2,128)}, u32[]{:S(2)}, u32[]{:S(2)}) async-start(f32[4,2,128,256]{3,1,2,0:T(2,128)} %broadcast_in_dim.21), calls=%async_computation.10 | async-start | bytes 2097152 | tf_op jit(solution)/shard_map/all_to_all | solution.py:42
  763.3 116.5 %all-reduce.23.cloned.1.call-start = ((), (), s32[]{:S(2)}) async-start(), calls=%async_computation.21 | async-start | bytes 4194304 | tf_op jit(solution)/shard_map/psum | solution.py:110
  812.7 67.0 %copy-start.6 = (f32[128,2048]{1,0:T(8,128)S(1)}, f32[128,2048]{1,0:T(8,128)}, u32[]{:S(2)}) copy-start(f32[128,2048]{1,0:T(8,128)} %copy-done.5) | copy-start | bytes 3145732
  812.7 33.0 %all-to-all-start.11 = ((f32[1,8,128,256]{3,2,0,1:T(8,128)}), f32[1,8,128,256]{3,2,0,1:T(8,128)S(1)}, u32[]{:S(2)}, u32[]{:S(2)}) async-start(f32[1,8,128,256]{3,2,0,1:T(8,128)} %bitcast.102), calls=%async_computation.11 | async-start | bytes 2097152 | tf_op jit(solution)/shard_map/all_to_all | solution.py:41
  882.4 1.0 copy-start.7
  882.4 59.4 %copy-start.2 = (f32[128,2048]{1,0:T(8,128)}, f32[128,2048]{1,0:T(8,128)S(1)}, u32[]{:S(2)}) copy-start(f32[128,2048]{1,0:T(8,128)S(1)} %get-tuple-element.12) | copy-start | bytes 3145732
  936.9 110.6 %all-to-all-start.13 = ((f32[1,8,128,512]{3,2,0,1:T(8,128)}), f32[1,8,128,512]{3,2,0,1:T(8,128)}, u32[]{:S(2)}, u32[]{:S(2)}) async-start(f32[1,8,128,512]{3,2,0,1:T(8,128)} %bitcast.31), calls=%async_computation.13 | async-start | bytes 4194304 | tf_op jit(solution)/shard_map/all_to_all | solution.py:20
  941.4 105.2 %all-reduce.19.cloned.1.call-start = ((), (), s32[]{:S(2)}) async-start(), calls=%async_computation.19 | async-start | bytes 4194304 | tf_op jit(solution)/shard_map/psum | solution.py:99
  1048.8 50.7 %all-to-all-start.14 = ((f32[4,2,128,256]{3,1,2,0:T(2,128)}), f32[4,2,128,256]{3,1,2,0:T(2,128)S(1)}, u32[]{:S(2)}, u32[]{:S(2)}) async-start(f32[4,2,128,256]{3,1,2,0:T(2,128)} %broadcast_in_dim.23), calls=%async_computation.14 | async-start | bytes 2097152 | tf_op jit(solution)/shard_map/all_to_all | solution.py:42
  1052.5 116.5 %all-reduce.21.cloned.1.call-start = ((), (), s32[]{:S(2)}) async-start(), calls=%async_computation.20 | async-start | bytes 4194304 | tf_op jit(solution)/shard_map/psum | solution.py:110
  1100.6 68.4 %copy-start.3 = (f32[128,2048]{1,0:T(8,128)S(1)}, f32[128,2048]{1,0:T(8,128)}, u32[]{:S(2)}) copy-start(f32[128,2048]{1,0:T(8,128)} %copy-done.2) | copy-start | bytes 3145732
  1100.6 68.4 %copy-start.8 = (f32[128,2048]{1,0:T(8,128)S(1)}, f32[128,2048]{1,0:T(8,128)}, u32[]{:S(2)}) copy-start(f32[128,2048]{1,0:T(8,128)} %copy-done.7) | copy-start | bytes 3145732
  1100.6 33.0 %all-to-all-start.15 = ((f32[1,8,128,256]{3,2,0,1:T(8,128)}), f32[1,8,128,256]{3,2,0,1:T(8,128)S(1)}, u32[]{:S(2)}, u32[]{:S(2)}) async-start(f32[1,8,128,256]{3,2,0,1:T(8,128)} %bitcast.103), calls=%async_computation.15 | async-start | bytes 2097152 | tf_op jit(solution)/shard_map/all_to_all | solution.py:41
Sparse Core Ops, SparseCore 0:
  110.4 64.4 all-reduce.12
  402.6 64.4 all-reduce.14
  692.3 64.4 all-reduce.16
  982.1 64.4 all-reduce.18
Sparse Core Ops, SparseCore 1:
  228.5 69.2 all-reduce.26
  521.0 69.2 all-reduce.24
  810.5 69.2 all-reduce.22
  1099.6 69.3 all-reduce.20
where the time goes:
time: 1190 us; the launch traced here: 1180 us
  waiting for transfers between devices  392 us (33%)
  blocking collectives  333 us (28%)
  matrix products  330 us (28%)
  starting transfers between devices  51 us (4%)
  local copies, waits for them, and re-layouts  43.7 us (4%)
  between operations  16.1 us (1%)
  other arithmetic  14.3 us (1%)
    psum x4, waiting for transfers between devices, body(): cross_total = lax.psum(part_cross, 'col')  258 us
    all_to_all x4, blocking collectives, turn_rows(): lax.all_to_all(spread, 'col', split_axis=0, concat_axis=1, tiled=True)  216 us
    dot_general x4, matrix products, body(): lax.dot_general(slope_contribution, hist_resp, (((1,), (1,)), ((), ())),...  151 us
    psum x4, waiting for transfers between devices, body(): memory_corr, memory_resp = lax.psum((part_corr, part_resp), 'row')  133 us
    psum x4, blocking collectives, body(): enforcing_scalar_sum = lax.psum(multiplier_terms, 'col')  117 us
    dot_general x4, matrix products, body(): jnp.dot(energy_rows, hist_resp, precision=highest, preferred_element_type...  89.7 us
    dot_general x4, matrix products, body(): jnp.dot(energy_rows, hist_corr, precision=highest, preferred_element_type...  89.7 us
  transfers between devices with their start and end apart: 20, of which 8 were waited for; matrix products, arithmetic and copies ran while one was open for 31% of the time, Pallas kernels for 0%

commit v1 on v0

--- a/solution.py
+++ b/solution.py
@@ -10,6 +10,28 @@
 heat_reservoir_warmth = 0.6
 
 
+def split_up(value, dim, count):
+    before, after = (value.shape[:dim], value.shape[dim + 1 :])
+    return jnp.moveaxis(value.reshape(*before, count, -1, *after), dim, 0)
+
+
+def in_order(parts, dim):
+    parts = jnp.moveaxis(parts, 0, dim)
+    shape = parts.shape
+    return parts.reshape(*shape[:dim], shape[dim] * shape[dim + 1], *shape[dim + 2 :])
+
+
+def sent_to_each(x, axis, split_dim, concat_dim):
+    size, place = (lax.axis_size(axis), lax.axis_index(axis))
+    blocks = split_up(x, split_dim, size)
+    finished = [blocks[place]]
+    for turn in range(1, size):
+        sent = blocks[(place + turn) % size]
+        finished.append(lax.ppermute(sent, axis, [(i, (i + turn) % size) for i in range(size)]))
+    blocks = jnp.stack(finished)[(place - jnp.arange(size)) % size]
+    return in_order(blocks, concat_dim)
+
+
 def turn_rows(values):
     row_count = lax.axis_size("row")
     col_count = lax.axis_size("col")
@@ -17,12 +39,8 @@
     piece_span = values.shape[1] // row_count
     piece = lax.dynamic_slice_in_dim(values, my_row * piece_span, piece_span, 1)
     spread = jnp.broadcast_to(piece[None, None], (col_count, 1) + piece.shape)
-    moved = lax.all_to_all(
-        lax.all_to_all(spread, "col", split_axis=0, concat_axis=1, tiled=True),
-        "row",
-        split_axis=1,
-        concat_axis=0,
-        tiled=True,
+    moved = sent_to_each(
+        lax.all_to_all(spread, "col", split_axis=0, concat_axis=1, tiled=True), "row", 1, 0
     )
     return jnp.transpose(moved, (2, 1, 0, 3)).reshape(piece.shape[0], -1)
 

time: 1190 us -> 1000 us (0.84)
  blocking collectives: 333 us -> 117 us
  local copies, waits for them, and re-layouts: 43.7 us -> 71.2 us
  waiting for transfers between devices: 392 us -> 374 us
  starting transfers between devices: 51 us -> 66.5 us
    all_to_all x4 -> x0, blocking collectives: 216 us -> none  [turn_rows(): lax.all_to_all(spread, 'col', split_axis=0, concat_axis=1, tiled=True)]
    psum x4, waiting for transfers between devices: 258 us -> 207 us  [body(): cross_total = lax.psum(part_cross, 'col')]
    all_to_all x4, waiting for transfers between devices: 0.01 us -> 32.5 us  [turn_rows(): lax.all_to_all(spread, 'col', split_axis=0, concat_axis=1, tiled=True)]
    ppermute x0 -> x12, starting transfers between devices: none -> 13.7 us  [sent_to_each(): lax.ppermute(sent, axis, [(i, (i + turn) % size) for i in range(size)])]
  transfers between devices with their start and end apart: 20 -> 32, of which waited for: 8 -> 12; matrix products, arithmetic and copies ran while one was open for 31% -> 40% of each run, Pallas kernels for 0% -> 0%
where the time goes in v1:
time: 1000 us; the launch traced here: 997 us
  waiting for transfers between devices  374 us (37%)
  matrix products  330 us (33%)
  blocking collectives  117 us (12%)
  local copies, waits for them, and re-layouts  71.2 us (7%)
  starting transfers between devices  66.5 us (7%)
  other arithmetic  21.5 us (2%)
  between operations  16.2 us (2%)
    psum x4, waiting for transfers between devices, body(): cross_total = lax.psum(part_cross, 'col')  207 us
    dot_general x4, matrix products, body(): lax.dot_general(slope_contribution, hist_resp, (((1,), (1,)), ((), ())),...  151 us
    psum x4, waiting for transfers between devices, body(): memory_corr, memory_resp = lax.psum((part_corr, part_resp), 'row')  134 us
    psum x4, blocking collectives, body(): enforcing_scalar_sum = lax.psum(multiplier_terms, 'col')  117 us
    dot_general x4, matrix products, body(): jnp.dot(energy_rows, hist_resp, precision=highest, preferred_element_type...  89.8 us
    dot_general x4, matrix products, body(): jnp.dot(energy_rows, hist_corr, precision=highest, preferred_element_type...  89.7 us
    all_to_all x4, waiting for transfers between devices, turn_rows(): lax.all_to_all(spread, 'col', split_axis=0, concat_axis=1, tiled=True)  32.5 us
    all_to_all x4, starting transfers between devices, turn_rows(): lax.all_to_all(spread, 'col', split_axis=0, concat_axis=1, tiled=True)  20.3 us
  transfers between devices with their start and end apart: 32, of which 12 were waited for; matrix products, arithmetic and copies ran while one was open for 40% of the time, Pallas kernels for 0%

profile of v1, /device:TPU:0, one launch (start us, length us, event | category | flops | bytes accessed | tf_op | source)
XLA Modules:
  0.0 996.8 jit_solution(3795585401593358550)
XLA Ops:
  11.6 6.5 all-to-all-start
  18.1 37.3 %fusion = f32[128,4096]{1,0:T(8,128)S(1)} fusion(f32[4096,2048]{1,0:T(8,128)} %param.5, f32[128,2048]{1,0:T(8,128)S(1)} %copy-done.4), kind=kOutput, calls=%fused_computation.28 | convolution fusion | flops 12885426176 | bytes 36700160 | tf_op jit(solution)/shard_map/dot_general | solution.py:108
  58.3 9.0 all-to-all-done
  73.5 51.4 %all-reduce.13.cloned.1.call-done = f32[128,2,2048]{2,1,0:T(2,128)} async-done(((f32[128,2,2048]{2,1,0:T(2,128)}), f32[128,2,2048]{2,1,0:T(2,128)}) %all-reduce.13.cloned.1.call-update) | async-done | bytes 2097168 | tf_op jit(solution)/shard_map/psum | solution.py:117
  138.4 22.4 %fusion.15 = f32[128,2048]{1,0:T(8,128)} fusion(f32[128,4096]{0,1:T(8,128)S(1)} %bitcast.118, f32[4096,2048]{1,0:T(8,128)} %param.5), kind=kOutput, calls=%fused_computation.76 | convolution fusion | flops 12884901888 | bytes 36700160 | tf_op jit(solution)/shard_map/dot_general | solution.py:125
  160.8 22.4 %fusion.14 = f32[128,2048]{1,0:T(8,128)} fusion(f32[128,4096]{0,1:T(8,128)S(1)} %bitcast.119, f32[4096,2048]{1,0:T(8,128)} %param.4), kind=kOutput, calls=%fused_computation.75 | convolution fusion | flops 12884901888 | bytes 36700160 | tf_op jit(solution)/shard_map/dot_general | solution.py:122
  189.3 29.3 %psum.114 = f32[128]{0:T(128)S(1)} all-reduce(f32[128]{0:T(128)S(1)} %get-tuple-element.36), channel_id=1, replica_groups=mesh['row'=4,'col'=8] {'col'}, use_global_device_ids=true, to_apply=%region_3.4 | all-reduce | flops 128 | bytes 1024 | tf_op jit(solution)/shard_map/psum | solution.py:115
  219.8 32.9 %all-reduce.27.cloned.1.call-done = (f32[128,2048]{1,0:T(8,128)}, f32[128,2048]{1,0:T(8,128)}) async-done(((f32[128,2048]{1,0:T(8,128)}, f32[128,2048]{1,0:T(8,128)}), (f32[128,2048]{1,0:T(8,128)}, f32[128,2048]{1,0:T(8,128)})) %all-reduce.27.cloned.1.call-update) | async-done | bytes 2097168 | tf_op jit(solution)/shard_map/psum | solution.py:128
  258.1 4.6 all-to-all-start.3
  263.0 39.0 %fusion.1 = f32[128,4096]{1,0:T(8,128)} fusion(f32[4096,2048]{1,0:T(8,128)} %param.5, f32[128,2048]{1,0:T(8,128)S(1)} %get-tuple-element.18), kind=kOutput, calls=%fused_computation.29 | convolution fusion | flops 12885426176 | bytes 36700160 | tf_op jit(solution)/shard_map/dot_general | solution.py:108
  306.0 5.9 all-to-all-done.3
  318.0 53.6 %all-reduce.15.cloned.1.call-done = f32[128,2,2048]{2,1,0:T(2,128)} async-done(((f32[128,2,2048]{2,1,0:T(2,128)}), f32[128,2,2048]{2,1,0:T(2,128)}) %all-reduce.15.cloned.1.call-update) | async-done | bytes 2097168 | tf_op jit(solution)/shard_map/psum | solution.py:117
  384.6 22.4 %fusion.17 = f32[128,2048]{1,0:T(8,128)} fusion(f32[128,4096]{0,1:T(8,128)S(1)} %bitcast.120, f32[4096,2048]{1,0:T(8,128)} %param.5), kind=kOutput, calls=%fused_computation.78 | convolution fusion | flops 12884901888 | bytes 36700160 | tf_op jit(solution)/shard_map/dot_general | solution.py:125
  407.1 22.4 %fusion.16 = f32[128,2048]{1,0:T(8,128)} fusion(f32[128,4096]{0,1:T(8,128)S(1)} %bitcast.121, f32[4096,2048]{1,0:T(8,128)} %param.4), kind=kOutput, calls=%fused_computation.77 | convolution fusion | flops 12884901888 | bytes 36700160 | tf_op jit(solution)/shard_map/dot_general | solution.py:122
  434.3 29.3 %psum.118 = f32[128]{0:T(128)S(1)} all-reduce(f32[128]{0:T(128)S(1)} %get-tuple-element.16), channel_id=1, replica_groups=mesh['row'=4,'col'=8] {'col'}, use_global_device_ids=true, to_apply=%region_8.9 | all-reduce | flops 128 | bytes 1024 | tf_op jit(solution)/shard_map/psum | solution.py:115
  464.7 34.2 %all-reduce.25.cloned.1.call-done = (f32[128,2048]{1,0:T(8,128)}, f32[128,2048]{1,0:T(8,128)}) async-done(((f32[128,2048]{1,0:T(8,128)}, f32[128,2048]{1,0:T(8,128)}), (f32[128,2048]{1,0:T(8,128)}, f32[128,2048]{1,0:T(8,128)})) %all-reduce.25.cloned.1.call-update) | async-done | bytes 2097168 | tf_op jit(solution)/shard_map/psum | solution.py:128
  503.8 4.6 all-to-all-start.6
  508.6 37.2 %fusion.2 = f32[128,4096]{1,0:T(8,128)S(1)} fusion(f32[4096,2048]{1,0:T(8,128)} %param.5, f32[128,2048]{1,0:T(8,128)S(1)} %get-tuple-element.15), kind=kOutput, calls=%fused_computation.30 | convolution fusion | flops 12885426176 | bytes 36700160 | tf_op jit(solution)/shard_map/dot_general | solution.py:108
  548.7 8.9 all-to-all-done.6
  563.7 50.8 %all-reduce.17.cloned.1.call-done = f32[128,2,2048]{2,1,0:T(2,128)} async-done(((f32[128,2,2048]{2,1,0:T(2,128)}), f32[128,2,2048]{2,1,0:T(2,128)}) %all-reduce.17.cloned.1.call-update) | async-done | bytes 2097168 | tf_op jit(solution)/shard_map/psum | solution.py:117
  628.0 22.5 %fusion.19 = f32[128,2048]{1,0:T(8,128)} fusion(f32[128,4096]{0,1:T(8,128)S(1)} %bitcast.122, f32[4096,2048]{1,0:T(8,128)} %param.5), kind=kOutput, calls=%fused_computation.80 | convolution fusion | flops 12884901888 | bytes 36700160 | tf_op jit(solution)/shard_map/dot_general | solution.py:125
  650.4 22.4 %fusion.18 = f32[128,2048]{1,0:T(8,128)} fusion(f32[128,4096]{0,1:T(8,128)S(1)} %bitcast.123, f32[4096,2048]{1,0:T(8,128)} %param.4), kind=kOutput, calls=%fused_computation.79 | convolution fusion | flops 12884901888 | bytes 36700160 | tf_op jit(solution)/shard_map/dot_general | solution.py:122
  678.9 29.3 %psum.122 = f32[128]{0:T(128)S(1)} all-reduce(f32[128]{0:T(128)S(1)} %get-tuple-element.13), channel_id=1, replica_groups=mesh['row'=4,'col'=8] {'col'}, use_global_device_ids=true, to_apply=%region_13.14 | all-reduce | flops 128 | bytes 1024 | tf_op jit(solution)/shard_map/psum | solution.py:115
  709.3 32.9 %all-reduce.23.cloned.1.call-done = (f32[128,2048]{1,0:T(8,128)}, f32[128,2048]{1,0:T(8,128)}) async-done(((f32[128,2048]{1,0:T(8,128)}, f32[128,2048]{1,0:T(8,128)}), (f32[128,2048]{1,0:T(8,128)}, f32[128,2048]{1,0:T(8,128)})) %all-reduce.23.cloned.1.call-update) | async-done | bytes 2097168 | tf_op jit(solution)/shard_map/psum | solution.py:128
  747.7 4.6 all-to-all-start.9
  752.8 37.2 %fusion.3 = f32[128,4096]{1,0:T(8,128)S(1)} fusion(f32[4096,2048]{1,0:T(8,128)} %param.5, f32[128,2048]{1,0:T(8,128)S(1)} %get-tuple-element.12), kind=kOutput, calls=%fused_computation.31 | convolution fusion | flops 12885426176 | bytes 36700160 | tf_op jit(solution)/shard_map/dot_general | solution.py:108
  792.8 8.7 all-to-all-done.9
  807.4 51.2 %all-reduce.19.cloned.1.call-done = f32[128,2,2048]{2,1,0:T(2,128)} async-done(((f32[128,2,2048]{2,1,0:T(2,128)}), f32[128,2,2048]{2,1,0:T(2,128)}) %all-reduce.19.cloned.1.call-update) | async-done | bytes 2097168 | tf_op jit(solution)/shard_map/psum | solution.py:117
  871.2 22.4 %fusion.21 = f32[128,2048]{1,0:T(8,128)} fusion(f32[128,4096]{0,1:T(8,128)S(1)} %bitcast.124, f32[4096,2048]{1,0:T(8,128)} %param.5), kind=kOutput, calls=%fused_computation.82 | convolution fusion | flops 12884901888 | bytes 36700160 | tf_op jit(solution)/shard_map/dot_general | solution.py:125
  893.6 22.4 %fusion.20 = f32[128,2048]{1,0:T(8,128)} fusion(f32[128,4096]{0,1:T(8,128)S(1)} %bitcast.125, f32[4096,2048]{1,0:T(8,128)} %param.4), kind=kOutput, calls=%fused_computation.81 | convolution fusion | flops 12884901888 | bytes 36700160 | tf_op jit(solution)/shard_map/dot_general | solution.py:122
  920.8 29.3 %psum.126 = f32[128]{0:T(128)S(1)} all-reduce(f32[128]{0:T(128)S(1)} %get-tuple-element.10), channel_id=1, replica_groups=mesh['row'=4,'col'=8] {'col'}, use_global_device_ids=true, to_apply=%region_18.19 | all-reduce | flops 128 | bytes 1024 | tf_op jit(solution)/shard_map/psum | solution.py:115
  951.3 34.3 %all-reduce.21.cloned.1.call-done = (f32[128,2048]{1,0:T(8,128)}, f32[128,2048]{1,0:T(8,128)}) async-done(((f32[128,2048]{1,0:T(8,128)}, f32[128,2048]{1,0:T(8,128)}), (f32[128,2048]{1,0:T(8,128)}, f32[128,2048]{1,0:T(8,128)})) %all-reduce.21.cloned.1.call-update) | async-done | bytes 2097168 | tf_op jit(solution)/shard_map/psum | solution.py:128
  (150 shorter events, 139.1 us)
Async XLA Ops:
  11.6 55.6 %all-to-all-start = ((f32[8,1,128,512]{3,2,1,0:T(8,128)}), f32[8,1,128,512]{3,2,1,0:T(8,128)}, u32[]{:S(2)}, u32[]{:S(2)}) async-start(f32[8,1,128,512]{3,2,1,0:T(8,128)} %broadcast_in_dim.16), calls=%async_computation | async-start | bytes 4194304 | tf_op jit(solution)/shard_map/all_to_all | solution.py:43
  18.1 106.9 %all-reduce.13.cloned.1.call-start = ((), (), s32[]{:S(2)}) async-start(), calls=%async_computation.12 | async-start | bytes 4194304 | tf_op jit(solution)/shard_map/psum | solution.py:117
  70.0 61.7 %collective-permute-start.2 = (f32[1,2,128,512]{3,2,1,0:T(8,128)}, f32[1,2,128,512]{3,2,1,0:T(8,128)S(1)}, u32[]{:S(2)}, u32[]{:S(2)}) collective-permute-start(f32[1,2,128,512]{3,2,1,0:T(8,128)} %get-tuple-element.32), channel_id=1, source_target_pairs={{0,24},{8,0},{16,8},{24,16},{1,25},{9,1},{17,9},{25,17},{2,26},{10... | collective-permute-start | bytes 1572872 | tf_op jit(solution)/shard_map/ppermute | solution.py:30
  72.4 59.3 %collective-permute-start.1 = (f32[1,2,128,512]{3,2,1,0:T(8,128)S(1)}, f32[1,2,128,512]{3,2,1,0:T(8,128)S(1)}, u32[]{:S(2)}, u32[]{:S(2)}) collective-permute-start(f32[1,2,128,512]{3,2,1,0:T(8,128)S(1)} %get-tuple-element.33), channel_id=1, source_target_pairs={{0,16},{8,24},{16,0},{24,8},{1,17},{9,25},{17,1},{25,9},{2,18},{10... | collective-permute-start | bytes 1572872 | tf_op jit(solution)/shard_map/ppermute | solution.py:30
  72.9 58.8 %collective-permute-start = (f32[1,2,128,512]{3,2,1,0:T(8,128)S(1)}, f32[1,2,128,512]{3,2,1,0:T(8,128)}, u32[]{:S(2)}, u32[]{:S(2)}) collective-permute-start(f32[1,2,128,512]{3,2,1,0:T(8,128)S(1)} %get-tuple-element.34), channel_id=1, source_target_pairs={{0,8},{8,16},{16,24},{24,0},{1,9},{9,17},{17,25},{25,1},{2,10},{10... | collective-permute-start | bytes 1572872 | tf_op jit(solution)/shard_map/ppermute | solution.py:30
  127.2 56.1 %all-to-all-start.1 = ((f32[4,2,128,256]{3,1,2,0:T(2,128)}), f32[4,2,128,256]{3,1,2,0:T(2,128)}, u32[]{:S(2)}, u32[]{:S(2)}) async-start(f32[4,2,128,256]{3,1,2,0:T(2,128)} %broadcast_in_dim.17), calls=%async_computation.1 | async-start | bytes 2097152 | tf_op jit(solution)/shard_map/all_to_all | solution.py:60
  131.5 121.2 %all-reduce.27.cloned.1.call-start = ((), (), s32[]{:S(2)}) async-start(), calls=%async_computation.19 | async-start | bytes 4194304 | tf_op jit(solution)/shard_map/psum | solution.py:128
  185.6 33.0 %all-to-all-start.2 = ((f32[1,8,128,256]{3,2,0,1:T(8,128)}), f32[1,8,128,256]{3,2,0,1:T(8,128)S(1)}, u32[]{:S(2)}, u32[]{:S(2)}) async-start(f32[1,8,128,256]{3,2,0,1:T(8,128)} %bitcast.13), calls=%async_computation.2 | async-start | bytes 2097152 | tf_op jit(solution)/shard_map/all_to_all | solution.py:59
  258.1 53.7 %all-to-all-start.3 = ((f32[8,1,128,512]{3,2,1,0:T(8,128)}), f32[8,1,128,512]{3,2,1,0:T(8,128)}, u32[]{:S(2)}, u32[]{:S(2)}) async-start(f32[8,1,128,512]{3,2,1,0:T(8,128)} %broadcast_in_dim.18), calls=%async_computation.3 | async-start | bytes 4194304 | tf_op jit(solution)/shard_map/all_to_all | solution.py:43
  262.7 108.9 %all-reduce.15.cloned.1.call-start = ((), (), s32[]{:S(2)}) async-start(), calls=%async_computation.13 | async-start | bytes 4194304 | tf_op jit(solution)/shard_map/psum | solution.py:117
  314.6 63.3 %collective-permute-start.5 = (f32[1,2,128,512]{3,2,1,0:T(8,128)}, f32[1,2,128,512]{3,2,1,0:T(8,128)S(1)}, u32[]{:S(2)}, u32[]{:S(2)}) collective-permute-start(f32[1,2,128,512]{3,2,1,0:T(8,128)} %get-tuple-element.28), channel_id=1, source_target_pairs={{0,24},{8,0},{16,8},{24,16},{1,25},{9,1},{17,9},{25,17},{2,26},{10... | collective-permute-start | bytes 1572872 | tf_op jit(solution)/shard_map/ppermute | solution.py:30
  316.2 61.7 %collective-permute-start.4 = (f32[1,2,128,512]{3,2,1,0:T(8,128)S(1)}, f32[1,2,128,512]{3,2,1,0:T(8,128)S(1)}, u32[]{:S(2)}, u32[]{:S(2)}) collective-permute-start(f32[1,2,128,512]{3,2,1,0:T(8,128)S(1)} %get-tuple-element.29), channel_id=1, source_target_pairs={{0,16},{8,24},{16,0},{24,8},{1,17},{9,25},{17,1},{25,9},{2,18},{10... | collective-permute-start | bytes 1572872 | tf_op jit(solution)/shard_map/ppermute | solution.py:30
  317.6 60.3 %collective-permute-start.3 = (f32[1,2,128,512]{3,2,1,0:T(8,128)S(1)}, f32[1,2,128,512]{3,2,1,0:T(8,128)}, u32[]{:S(2)}, u32[]{:S(2)}) collective-permute-start(f32[1,2,128,512]{3,2,1,0:T(8,128)S(1)} %get-tuple-element.30), channel_id=1, source_target_pairs={{0,8},{8,16},{16,24},{24,0},{1,9},{9,17},{17,25},{25,1},{2,10},{10... | collective-permute-start | bytes 1572872 | tf_op jit(solution)/shard_map/ppermute | solution.py:30
  373.8 55.7 %all-to-all-start.4 = ((f32[4,2,128,256]{3,1,2,0:T(2,128)}), f32[4,2,128,256]{3,1,2,0:T(2,128)S(1)}, u32[]{:S(2)}, u32[]{:S(2)}) async-start(f32[4,2,128,256]{3,1,2,0:T(2,128)} %broadcast_in_dim.19), calls=%async_computation.4 | async-start | bytes 2097152 | tf_op jit(solution)/shard_map/all_to_all | solution.py:60
  377.5 121.5 %all-reduce.25.cloned.1.call-start = ((), (), s32[]{:S(2)}) async-start(), calls=%async_computation.18 | async-start | bytes 4194304 | tf_op jit(solution)/shard_map/psum | solution.py:128
  430.6 33.0 %all-to-all-start.5 = ((f32[1,8,128,256]{3,2,0,1:T(8,128)}), f32[1,8,128,256]{3,2,0,1:T(8,128)S(1)}, u32[]{:S(2)}, u32[]{:S(2)}) async-start(f32[1,8,128,256]{3,2,0,1:T(8,128)} %bitcast.134), calls=%async_computation.5 | async-start | bytes 2097152 | tf_op jit(solution)/shard_map/all_to_all | solution.py:59
  503.8 53.8 %all-to-all-start.6 = ((f32[8,1,128,512]{3,2,1,0:T(8,128)}), f32[8,1,128,512]{3,2,1,0:T(8,128)}, u32[]{:S(2)}, u32[]{:S(2)}) async-start(f32[8,1,128,512]{3,2,1,0:T(8,128)} %broadcast_in_dim.20), calls=%async_computation.6 | async-start | bytes 4194304 | tf_op jit(solution)/shard_map/all_to_all | solution.py:43
  508.4 106.1 %all-reduce.17.cloned.1.call-start = ((), (), s32[]{:S(2)}) async-start(), calls=%async_computation.14 | async-start | bytes 4194304 | tf_op jit(solution)/shard_map/psum | solution.py:117
  560.3 60.9 %collective-permute-start.8 = (f32[1,2,128,512]{3,2,1,0:T(8,128)}, f32[1,2,128,512]{3,2,1,0:T(8,128)S(1)}, u32[]{:S(2)}, u32[]{:S(2)}) collective-permute-start(f32[1,2,128,512]{3,2,1,0:T(8,128)} %get-tuple-element.24), channel_id=1, source_target_pairs={{0,24},{8,0},{16,8},{24,16},{1,25},{9,1},{17,9},{25,17},{2,26},{10... | collective-permute-start | bytes 1572872 | tf_op jit(solution)/shard_map/ppermute | solution.py:30
  561.7 59.5 %collective-permute-start.7 = (f32[1,2,128,512]{3,2,1,0:T(8,128)S(1)}, f32[1,2,128,512]{3,2,1,0:T(8,128)S(1)}, u32[]{:S(2)}, u32[]{:S(2)}) collective-permute-start(f32[1,2,128,512]{3,2,1,0:T(8,128)S(1)} %get-tuple-element.25), channel_id=1, source_target_pairs={{0,16},{8,24},{16,0},{24,8},{1,17},{9,25},{17,1},{25,9},{2,18},{10... | collective-permute-start | bytes 1572872 | tf_op jit(solution)/shard_map/ppermute | solution.py:30
  563.3 58.0 %collective-permute-start.6 = (f32[1,2,128,512]{3,2,1,0:T(8,128)S(1)}, f32[1,2,128,512]{3,2,1,0:T(8,128)}, u32[]{:S(2)}, u32[]{:S(2)}) collective-permute-start(f32[1,2,128,512]{3,2,1,0:T(8,128)S(1)} %get-tuple-element.26), channel_id=1, source_target_pairs={{0,8},{8,16},{16,24},{24,0},{1,9},{9,17},{17,25},{25,1},{2,10},{10... | collective-permute-start | bytes 1572872 | tf_op jit(solution)/shard_map/ppermute | solution.py:30
  616.7 56.2 %all-to-all-start.7 = ((f32[4,2,128,256]{3,1,2,0:T(2,128)}), f32[4,2,128,256]{3,1,2,0:T(2,128)}, u32[]{:S(2)}, u32[]{:S(2)}) async-start(f32[4,2,128,256]{3,1,2,0:T(2,128)} %broadcast_in_dim.21), calls=%async_computation.7 | async-start | bytes 2097152 | tf_op jit(solution)/shard_map/all_to_all | solution.py:60
  620.9 121.3 %all-reduce.23.cloned.1.call-start = ((), (), s32[]{:S(2)}) async-start(), calls=%async_computation.17 | async-start | bytes 4194304 | tf_op jit(solution)/shard_map/psum | solution.py:128
  675.2 33.0 %all-to-all-start.8 = ((f32[1,8,128,256]{3,2,0,1:T(8,128)}), f32[1,8,128,256]{3,2,0,1:T(8,128)S(1)}, u32[]{:S(2)}, u32[]{:S(2)}) async-start(f32[1,8,128,256]{3,2,0,1:T(8,128)} %bitcast.135), calls=%async_computation.8 | async-start | bytes 2097152 | tf_op jit(solution)/shard_map/all_to_all | solution.py:59
  747.7 53.8 %all-to-all-start.9 = ((f32[8,1,128,512]{3,2,1,0:T(8,128)}), f32[8,1,128,512]{3,2,1,0:T(8,128)}, u32[]{:S(2)}, u32[]{:S(2)}) async-start(f32[8,1,128,512]{3,2,1,0:T(8,128)} %broadcast_in_dim.22), calls=%async_computation.9 | async-start | bytes 4194304 | tf_op jit(solution)/shard_map/all_to_all | solution.py:43
  752.3 106.3 %all-reduce.19.cloned.1.call-start = ((), (), s32[]{:S(2)}) async-start(), calls=%async_computation.15 | async-start | bytes 4194304 | tf_op jit(solution)/shard_map/psum | solution.py:117
  804.1 60.6 %collective-permute-start.11 = (f32[1,2,128,512]{3,2,1,0:T(8,128)S(1)}, f32[1,2,128,512]{3,2,1,0:T(8,128)S(1)}, u32[]{:S(2)}, u32[]{:S(2)}) collective-permute-start(f32[1,2,128,512]{3,2,1,0:T(8,128)S(1)} %get-tuple-element.20), channel_id=1, source_target_pairs={{0,24},{8,0},{16,8},{24,16},{1,25},{9,1},{17,9},{25,17},{2,26},{10... | collective-permute-start | bytes 1572872 | tf_op jit(solution)/shard_map/ppermute | solution.py:30
  805.5 59.2 %collective-permute-start.10 = (f32[1,2,128,512]{3,2,1,0:T(8,128)S(1)}, f32[1,2,128,512]{3,2,1,0:T(8,128)}, u32[]{:S(2)}, u32[]{:S(2)}) collective-permute-start(f32[1,2,128,512]{3,2,1,0:T(8,128)S(1)} %get-tuple-element.21), channel_id=1, source_target_pairs={{0,16},{8,24},{16,0},{24,8},{1,17},{9,25},{17,1},{25,9},{2,18},{10... | collective-permute-start | bytes 1572872 | tf_op jit(solution)/shard_map/ppermute | solution.py:30
  807.0 57.7 %collective-permute-start.9 = (f32[1,2,128,512]{3,2,1,0:T(8,128)S(1)}, f32[1,2,128,512]{3,2,1,0:T(8,128)}, u32[]{:S(2)}, u32[]{:S(2)}) collective-permute-start(f32[1,2,128,512]{3,2,1,0:T(8,128)S(1)} %get-tuple-element.22), channel_id=1, source_target_pairs={{0,8},{8,16},{16,24},{24,0},{1,9},{9,17},{17,25},{25,1},{2,10},{10... | collective-permute-start | bytes 1572872 | tf_op jit(solution)/shard_map/ppermute | solution.py:30
  860.8 55.3 %all-to-all-start.10 = ((f32[4,2,128,256]{3,1,2,0:T(2,128)}), f32[4,2,128,256]{3,1,2,0:T(2,128)S(1)}, u32[]{:S(2)}, u32[]{:S(2)}) async-start(f32[4,2,128,256]{3,1,2,0:T(2,128)} %broadcast_in_dim.23), calls=%async_computation.10 | async-start | bytes 2097152 | tf_op jit(solution)/shard_map/all_to_all | solution.py:60
  864.4 121.1 %all-reduce.21.cloned.1.call-start = ((), (), s32[]{:S(2)}) async-start(), calls=%async_computation.16 | async-start | bytes 4194304 | tf_op jit(solution)/shard_map/psum | solution.py:128
  917.1 33.0 %all-to-all-start.11 = ((f32[1,8,128,256]{3,2,0,1:T(8,128)}), f32[1,8,128,256]{3,2,0,1:T(8,128)S(1)}, u32[]{:S(2)}, u32[]{:S(2)}) async-start(f32[1,8,128,256]{3,2,0,1:T(8,128)} %bitcast.136), calls=%async_computation.11 | async-start | bytes 2097152 | tf_op jit(solution)/shard_map/all_to_all | solution.py:59
  (18 other events, 371.3 us)
Sparse Core Ops, SparseCore 0:
  58.3 66.5 all-reduce.12
  306.1 65.4 all-reduce.14
  548.8 65.6 all-reduce.16
  793.0 65.5 all-reduce.18
Sparse Core Ops, SparseCore 1:
  183.4 69.2 all-reduce.26
  429.6 69.3 all-reduce.24
  673.0 69.2 all-reduce.22
  916.1 69.3 all-reduce.20
